TPU v7x, 512 devices: a whole 4x4x16 slice. The times are simulated.
512 devices in a mesh: row: 16 (over y, x), adp: 32 (over z, core).
Axes of the slice: x: 4, y: 4, z: 16, core: 2. Of those that a mesh axis runs over, the one named last changes fastest.
Arguments:
- tokens: bfloat16 [8192, 8192], P('row', 'adp'), may hold values from -6 to 6
- query_base_weight: bfloat16 [8192, 8192], P(None, 'adp'), may hold values from -0.0625 to 0.0625
- adapter_down_weight: bfloat16 [32, 16, 8192], P('adp'), may hold values from -0.0625 to 0.0625
- adapter_up_weight: bfloat16 [32, 16, 8192], P('adp'), may hold values from -1.5 to 1.5
- row_adapter_index: int32 [8192, 1], P('row'), may hold values from 0 to 31; in each aligned block of 512 rows (0 to 511, 512 to 1023, ...) at most 64 rows name the same one
Outputs:
- queries: bfloat16 [8192, 8192], P('row', 'adp')
Inputs may be any that keep to these rules, and one draw needn't show every extreme that they name: `row_adapter_index`: among the 512 rows of one index of row, no adapter is used by more than 64 rows, and some adapter is used by exactly 64 rows; every adapter is used by some row.
All inputs are finite; a program needn't handle non-finite values.
Results may differ from a plain program's by a relative error of at most 0.0055.
Values may be sent and summed in bfloat16 or wider, within the bound.
No kernel may reach another device: no remote copies, remote signals or barrier semaphores. Data moves between devices by JAX's collectives and lax.ppermute only.
A program may use at most 64 MiB of HBM per device.

v0:
```python
import jax
import jax.numpy as jnp
from jax import lax
from jax.sharding import PartitionSpec as P

ADAPTER_RANK = 16
SCALE_NUMERATOR = 32


def shards(tokens, query_base_weight, adapter_down_weight, adapter_up_weight, row_adapter_index):
    row_count = tokens.shape[0]
    total_width = query_base_weight.shape[0]
    local_row_count = adapter_down_weight.shape[0]
    rank_length = adapter_down_weight.shape[1]
    groups = lax.axis_size("adp")
    total_adapters = local_row_count * groups
    capacity = 4 * row_count // total_adapters
    position = lax.axis_index("adp")
    adapter_scale = SCALE_NUMERATOR / ADAPTER_RANK
    down_weight_flat = adapter_down_weight.reshape(local_row_count * rank_length, total_width)
    shard_piece = lax.all_gather(tokens, "adp", axis=1, tiled=True)
    base_part = jnp.dot(shard_piece, query_base_weight, preferred_element_type=jnp.float32)
    down_part = lax.dot_general(
        shard_piece, down_weight_flat, (((1,), (1,)), ((), ())), preferred_element_type=jnp.float32
    )
    adapter_of = row_adapter_index[:, 0]
    every_match = adapter_of[:, None] == jnp.arange(total_adapters, dtype=jnp.int32)[None, :]
    owned_match = lax.dynamic_slice_in_dim(
        every_match, position * local_row_count, local_row_count, 1
    )
    rank_own = jnp.where(
        jnp.repeat(owned_match, rank_length, axis=1), down_part, jnp.zeros_like(down_part)
    ).astype(jnp.bfloat16)
    order_in = jnp.cumsum(every_match.astype(jnp.int32), axis=0) - 1
    slot_index = jnp.arange(capacity, dtype=jnp.int32)
    slot_table = (
        every_match.T[:, None, :] & (order_in.T[:, None, :] == slot_index[None, :, None])
    ).astype(jnp.bfloat16)
    own_table = lax.dynamic_slice_in_dim(slot_table, position * local_row_count, local_row_count, 0)
    selected_rows = jnp.einsum(
        "acn,nak->ack",
        own_table,
        rank_own.reshape(row_count, local_row_count, rank_length),
        preferred_element_type=jnp.float32,
    ).astype(jnp.bfloat16)
    update_rows = (
        jnp.einsum(
            "vbf,vfx->vbx", selected_rows, adapter_up_weight, preferred_element_type=jnp.float32
        )
        * adapter_scale
    ).astype(jnp.bfloat16)
    arrived = lax.all_to_all(
        update_rows.reshape(local_row_count * capacity, total_width),
        "adp",
        split_axis=1,
        concat_axis=0,
        tiled=True,
    )
    update = lax.dot_general(
        slot_table.reshape(total_adapters * capacity, row_count),
        arrived,
        (((0,), (0,)), ((), ())),
        preferred_element_type=jnp.float32,
    ).astype(jnp.bfloat16)
    update = lax.optimization_barrier(update)
    return (base_part + update.astype(jnp.float32)).astype(jnp.bfloat16)


def solution(mesh):
    return jax.shard_map(
        shards,
        mesh=mesh,
        in_specs=(
            P("row", "adp"),
            P(None, "adp"),
            P("adp", None, None),
            P("adp", None, None),
            P("row", None),
        ),
        out_specs=P("row", "adp"),
        check_vma=False,
    )
```

profile of v0, /device:TPU:1, one launch (start us, length us, event | category | flops | bytes accessed | tf_op | source)
XLA Modules:
  0.0 193.7 jit_solution(11247434372727005446)
XLA Ops:
  6.5 0.0 copy-start
  6.5 0.0 all-gather.2.cloned.1.call-start
  6.5 0.7 all-gather.2.cloned.1.call-update
  7.3 0.7 fusion.15
  8.0 1.2 reduce-window.6
  9.1 0.2 slice_reduce_fusion
  9.4 0.7 compare_reduce_fusion
  10.1 0.7 iota_compare_fusion.2
  10.8 0.1 copy_bitcast_fusion.1
  10.9 0.9 fusion.1
  11.8 98.9 %all-gather.2.cloned.1.call-done = bf16[512,8192]{1,0:T(8,128)(2,1)} async-done(((bf16[512,256]{1,0:T(8,128)(2,1)}), bf16[512,8192]{1,0:T(8,128)(2,1)}) %all-gather.2.cloned.1.call-update) | async-done | bytes 8388624 | tf_op jit(solution)/shard_map/all_gather | solution.py:21
  110.7 5.8 %fusion.6 = bf16[64,16]{1,0:T(8,128)(2,1)S(1)} fusion(bf16[512,8192]{1,0:T(8,128)(2,1)} %all-gather.2.cloned.1.call-done, bf16[1,16,8192]{2,1,0:T(8,128)(2,1)} %param.7, pred[512]{0:T(512)(128)(4,1)S(1)} %compare_reduce_fusion, pred[32,64,512]{2,1,0:T(32,128)(4,1)S(1)} %fusion.1, s32[]{:T(128)S(6)} %select_n.8), kind=kOutput, calls=%fused_computation.11 | convolution fusion | flops 135283712 | bytes 8686084 | tf_op jit(solution)/shard_map/acn,nak->ack/dot_general | solution.py:40
  116.5 0.0 copy-done
  116.5 0.4 fusion
  117.0 0.0 slice-start
  117.0 0.1 copy.13
  117.1 63.3 %all_to_all.16 = bf16[64,32,256]{2,0,1:T(8,128)(2,1)S(1)} all-to-all(bf16[64,32,256]{2,0,1:T(8,128)(2,1)S(1)} %bitcast.33), channel_id=1, replica_groups=mesh['row'=16,'adp'=32] {'adp'}, dimensions={1} | all-to-all | bytes 2097152 | tf_op jit(solution)/shard_map/all_to_all | solution.py:52
  180.4 0.0 slice-start.1
  180.4 0.0 copy-start.1
  180.4 1.3 fusion.3
  181.7 0.0 slice-done
  181.7 0.9 slice-done.1
  182.6 1.3 copy-done.1
  183.8 3.0 %fusion.2 = bf16[512,256]{1,0:T(8,128)(2,1)} fusion(bf16[512,8192]{1,0:T(8,128)(2,1)S(1)} %bitcast.38, bf16[8192,256]{1,0:T(8,128)(2,1)S(1)} %copy-done.1, bf16[512,256]{1,0:T(8,128)(2,1)S(1)} %fusion.3), kind=kOutput, calls=%fused_computation.6 | convolution fusion | flops 2147876864 | bytes 13107200 | tf_op jit(solution)/shard_map/dot_general | solution.py:22
  (3 shorter events, 0.0 us)
Async XLA Ops:
  6.5 110.0 %copy-start = (bf16[1,16,8192]{2,1,0:T(8,128)(2,1)S(1)}, bf16[1,16,8192]{2,1,0:T(8,128)(2,1)}, u32[]{:S(2)}) copy-start(bf16[1,16,8192]{2,1,0:T(8,128)(2,1)} %param.8) | copy-start | bytes 786436
  6.5 104.2 %all-gather.2.cloned.1.call-start = ((), (), s32[]{:S(2)}) async-start(), calls=%async_computation.1 | async-start | bytes 8650752 | tf_op jit(solution)/shard_map/all_gather | solution.py:21
  117.0 64.7 %slice-start = ((s8[8388608]{0:T(1024)(128)(4,1)}), s8[4194304]{0:T(1024)(128)(4,1)S(1)}, s32[]{:S(2)}) async-start(s8[8388608]{0:T(1024)(128)(4,1)} %bitcast.37), calls=%async_computation.2 | async-start | bytes 8388608
  180.4 2.2 %slice-start.1 = ((s8[8388608]{0:T(1024)(128)(4,1)}), s8[4194304]{0:T(1024)(128)(4,1)S(1)}, s32[]{:S(2)}) async-start(s8[8388608]{0:T(1024)(128)(4,1)} %bitcast.37), calls=%async_computation.3 | async-start | bytes 8388608
  180.4 3.5 %copy-start.1 = (bf16[8192,256]{1,0:T(8,128)(2,1)S(1)}, bf16[8192,256]{1,0:T(8,128)(2,1)}, u32[]{:S(2)}) copy-start(bf16[8192,256]{1,0:T(8,128)(2,1)} %param.6) | copy-start | bytes 12582916
Sparse Core Ops, SparseCore 0:
  9.4 101.2 all-gather.1
where the time goes:
time: 194 us
  waiting for transfers between devices  99.6 us (51%)
  blocking collectives  63.3 us (33%)
  between operations  13.5 us (7%)
  matrix products  10.6 us (5%)
  other arithmetic  4.29 us (2%)
  local copies, waits for them, and re-layouts  2.49 us (1%)
    all_gather x1, waiting for transfers between devices, shards(): shard_piece = lax.all_gather(tokens, 'adp', axis=1, tiled=True)  98.9 us
    all_to_all x1, blocking collectives, shards(): lax.all_to_all(update_rows.reshape(local_row_count * capacity, total_widt...  63.3 us
    dot_general x1, matrix products, shards(): jnp.einsum('acn,nak->ack', own_table, rank_own.reshape(row_count, local_r...  5.83 us
  transfers between devices with their start and end apart: 1, of which 1 were waited for; matrix products, arithmetic and copies ran while one was open for 2% of the time, Pallas kernels for 0%

commit v1 on v0

--- a/solution.py
+++ b/solution.py
@@ -18,7 +18,9 @@
     position = lax.axis_index("adp")
     adapter_scale = SCALE_NUMERATOR / ADAPTER_RANK
     down_weight_flat = adapter_down_weight.reshape(local_row_count * rank_length, total_width)
-    shard_piece = lax.all_gather(tokens, "adp", axis=1, tiled=True)
+    shard_piece = jnp.concatenate(
+        lax.all_to_all(jnp.stack([tokens] * lax.axis_size("adp")), "adp", 0, 0), axis=1
+    )
     base_part = jnp.dot(shard_piece, query_base_weight, preferred_element_type=jnp.float32)
     down_part = lax.dot_general(
         shard_piece, down_weight_flat, (((1,), (1,)), ((), ())), preferred_element_type=jnp.float32

time: 194 us -> 466 us (2.40)
  waiting for transfers between devices: 99.6 us -> 358 us
  starting transfers between devices: 0.01 us -> 16.9 us
  between operations: 13.5 us -> 0.1 us
  blocking collectives: 63.3 us -> 68.3 us
    all_to_all x0 -> x1, waiting for transfers between devices: none -> 358 us  [shards(): lax.all_to_all(jnp.stack([tokens] * lax.axis_size('adp')), 'adp', 0, 0)]
    all_gather x1 -> x0, waiting for transfers between devices: 98.9 us -> none  [shards(): shard_piece = lax.all_gather(tokens, 'adp', axis=1, tiled=True)]
    all_to_all x0 -> x1, starting transfers between devices: none -> 16.9 us  [shards(): lax.all_to_all(jnp.stack([tokens] * lax.axis_size('adp')), 'adp', 0, 0)]
    all_to_all x1, blocking collectives: 63.3 us -> 68.3 us  [shards(): lax.all_to_all(update_rows.reshape(local_row_count * capacity, total_widt...]
  transfers between devices with their start and end apart: 1 -> 1, of which waited for: 1 -> 1; matrix products, arithmetic and copies ran while one was open for 2% -> 1% of each run, Pallas kernels for 0% -> 0%
where the time goes in v1:
time: 466 us
  waiting for transfers between devices  358 us (77%)
  blocking collectives  68.3 us (15%)
  starting transfers between devices  16.9 us (4%)
  matrix products  14.1 us (3%)
  local copies, waits for them, and re-layouts  6.51 us (1%)
    all_to_all x1, waiting for transfers between devices, shards(): lax.all_to_all(jnp.stack([tokens] * lax.axis_size('adp')), 'adp', 0, 0)  358 us
    all_to_all x1, blocking collectives, shards(): lax.all_to_all(update_rows.reshape(local_row_count * capacity, total_widt...  68.3 us
    all_to_all x1, starting transfers between devices, shards(): lax.all_to_all(jnp.stack([tokens] * lax.axis_size('adp')), 'adp', 0, 0)  16.9 us
  transfers between devices with their start and end apart: 1, of which 1 were waited for; matrix products, arithmetic and copies ran while one was open for 1% of the time, Pallas kernels for 0%

profile of v1, /device:TPU:1, one launch (start us, length us, event | category | flops | bytes accessed | tf_op | source)
XLA Modules:
  0.0 466.2 jit_solution(11368300762481408209)
XLA Ops:
  0.0 0.0 copy-start
  0.0 1.1 copy.7
  1.1 4.2 stack.2
  5.3 0.0 copy-start.2
  5.3 0.0 copy-start.3
  5.3 16.9 %all-to-all-start = ((bf16[32,512,256]{1,2,0:T(8,128)(2,1)}), bf16[32,512,256]{1,2,0:T(8,128)(2,1)}, u32[]{:S(2)}, u32[]{:S(2)}) async-start(bf16[32,512,256]{1,2,0:T(8,128)(2,1)} %stack.2), calls=%async_computation | async-start | bytes 16777216 | tf_op jit(solution)/shard_map/all_to_all | solution.py:22
  22.2 0.0 copy-done.2
  22.3 1.2 reduce-window.6
  23.4 0.2 slice_reduce_fusion
  23.7 0.1 copy_bitcast_fusion.1
  23.8 0.9 fusion.1
  24.8 358.1 %all-to-all-done = bf16[32,512,256]{1,2,0:T(8,128)(2,1)} async-done(((bf16[32,512,256]{1,2,0:T(8,128)(2,1)}), bf16[32,512,256]{1,2,0:T(8,128)(2,1)}, u32[]{:S(2)}, u32[]{:S(2)}) %all-to-all-start) | async-done | bytes 8388640 | tf_op jit(solution)/shard_map/all_to_all | solution.py:22
  382.8 0.0 copy-done.3
  382.8 5.9 %fusion.6 = bf16[64,16]{1,0:T(8,128)(2,1)S(1)} fusion(bf16[512,8192]{0,1:T(8,128)(2,1)} %bitcast.1, bf16[1,16,8192]{2,1,0:T(8,128)(2,1)S(1)} %copy-done.3, pred[512]{0:T(512)(128)(4,1)S(1)} %compare_reduce_fusion, pred[32,64,512]{2,1,0:T(32,128)(4,1)S(1)} %fusion.1, s32[]{:T(128)S(6)} %select_n.8), kind=kOutput, calls=%fused_computation.11 | convolution fusion | flops 135283712 | bytes 8686084 | tf_op jit(solution)/shard_map/acn,nak->ack/dot_general | solution.py:42
  388.7 0.0 copy-done
  388.7 0.4 fusion
  389.1 0.1 copy.14
  389.2 68.3 %all_to_all.21 = bf16[64,32,256]{2,0,1:T(8,128)(2,1)S(1)} all-to-all(bf16[64,32,256]{2,0,1:T(8,128)(2,1)S(1)} %bitcast.36), channel_id=1, replica_groups=mesh['row'=16,'adp'=32] {'adp'}, dimensions={1} | all-to-all | bytes 2097152 | tf_op jit(solution)/shard_map/all_to_all | solution.py:54
  457.5 0.0 copy-start.1
  457.5 1.3 fusion.2
  458.8 0.9 copy-done.1
  459.7 6.5 %fusion.3 = bf16[512,256]{1,0:T(8,128)(2,1)} fusion(bf16[512,8192]{0,1:T(8,128)(2,1)} %bitcast.1, bf16[8192,256]{1,0:T(8,128)(2,1)S(1)} %copy-done.1, bf16[512,256]{1,0:T(8,128)(2,1)S(1)} %fusion.2), kind=kOutput, calls=%fused_computation.7 | convolution fusion | flops 2147876864 | bytes 13107200 | tf_op jit(solution)/shard_map/dot_general | solution.py:24
  (5 shorter events, 0.1 us)
Async XLA Ops:
  0.0 388.7 %copy-start = (bf16[1,16,8192]{2,1,0:T(8,128)(2,1)S(1)}, bf16[1,16,8192]{2,1,0:T(8,128)(2,1)}, u32[]{:S(2)}) copy-start(bf16[1,16,8192]{2,1,0:T(8,128)(2,1)} %param.8) | copy-start | bytes 786436
  5.3 16.9 %copy-start.2 = (s32[512,1]{0,1:T(1,128)S(1)}, s32[512,1]{0,1:T(1,128)}, u32[]{:S(2)}) copy-start(s32[512,1]{0,1:T(1,128)} %param.9) | copy-start | bytes 6148
  5.3 377.5 %copy-start.3 = (bf16[1,16,8192]{2,1,0:T(8,128)(2,1)S(1)}, bf16[1,16,8192]{2,1,0:T(8,128)(2,1)}, u32[]{:S(2)}) copy-start(bf16[1,16,8192]{2,1,0:T(8,128)(2,1)} %param.7) | copy-start | bytes 786436
  5.3 377.5 %all-to-all-start = ((bf16[32,512,256]{1,2,0:T(8,128)(2,1)}), bf16[32,512,256]{1,2,0:T(8,128)(2,1)}, u32[]{:S(2)}, u32[]{:S(2)}) async-start(bf16[32,512,256]{1,2,0:T(8,128)(2,1)} %stack.2), calls=%async_computation | async-start | bytes 16777216 | tf_op jit(solution)/shard_map/all_to_all | solution.py:22
  457.5 2.2 copy-start.1
